TPU v7x, 512 devices: a whole 4x8x8 slice. The times are simulated.
512 devices in a mesh: slab: 128 (over z, y, core), chan: 4 (over x).
Axes of the slice: x: 4, y: 8, z: 8, core: 2. Of those that a mesh axis runs over, the one named last changes fastest.
Arguments:
- field: bfloat16 [64, 256, 4096], P(None, 'slab'), may hold values from -6 to 6
- cotangent: bfloat16 [64, 256, 4096], P(None, 'slab'), may hold values from -10 to 10
- spectral_weight: bfloat16 [2, 64, 64, 512, 32], P(None, 'chan', None, 'slab'), may hold values from -4 to 4
- point_weight: bfloat16 [64, 64], replicated, may hold values from -0.75 to 0.75
- point_bias: bfloat16 [64], replicated, may hold values from -2 to 2
Outputs:
- grad_input: bfloat16 [64, 256, 4096], P('chan', 'slab')
- grad_spectral: float32 [2, 64, 64, 512, 32], P(None, 'chan', None, 'slab')
- grad_pointwise: float32 [64, 64], P('chan')
- grad_bias: float32 [64], replicated
All inputs are finite; a program needn't handle non-finite values.
Results may differ from a plain program's by a relative error of at most 0.023.
Values may be sent and summed in bfloat16 or wider, within the bound.
No kernel may reach another device: no remote copies, remote signals or barrier semaphores. Data moves between devices by JAX's collectives and lax.ppermute only.
A program may use at most 64 MiB of HBM per device.

v0:
```python
import math
import jax
import jax.numpy as jnp
from jax import lax
from jax.sharding import PartitionSpec as P

MX = 32
MY = 32
MZ = 16
NX = 256
NY = 64
NZ = 64


def kept_modes(total, length):
    mode_index = jnp.arange(total, dtype=jnp.int32)
    return jnp.where(mode_index < total // 2, mode_index, mode_index - total + length)


def phases(frequency, length):
    positions = jnp.arange(length, dtype=jnp.int32)
    wound_up = frequency[:, None] * positions[None, :] % length
    return 2.0 * math.pi / length * wound_up.astype(jnp.float32)


def make_tables():
    angle_z = phases(jnp.arange(MZ, dtype=jnp.int32), NZ)
    cosine_z = jnp.cos(angle_z)
    sine_z = jnp.sin(angle_z)
    forward_z = jnp.stack([cosine_z.T, -sine_z.T], 1).astype(jnp.bfloat16)
    weight_z = (jnp.where(jnp.arange(MZ) == 0, 1.0, 2.0) / (NX * NY * NZ)).astype(jnp.float32)
    scaled_z = jnp.stack([weight_z[:, None] * cosine_z, -weight_z[:, None] * sine_z], 1).astype(
        jnp.bfloat16
    )
    plain_z = jnp.stack([cosine_z, -sine_z], 1).astype(jnp.bfloat16)
    angle_y = phases(kept_modes(MY, NY), NY)
    cosine_y = jnp.cos(angle_y)
    sine_y = jnp.sin(angle_y)
    upper_rows = jnp.stack([cosine_y.T, -sine_y.T], -1)
    lower_rows = jnp.stack([sine_y.T, cosine_y.T], -1)
    forward_y = jnp.stack([upper_rows, lower_rows], 0).reshape(2 * NY, 2 * MY).astype(jnp.bfloat16)
    real_rows = jnp.stack([cosine_y, sine_y], 1)
    imag_rows = jnp.stack([-sine_y, cosine_y], 1)
    inverse_y = jnp.stack([real_rows, imag_rows], 1).reshape(2 * MY, 2 * NY).astype(jnp.bfloat16)
    angle_x = phases(kept_modes(MX, NX), NX)
    cosine_x = jnp.cos(angle_x).T.astype(jnp.bfloat16)
    sine_x = jnp.sin(angle_x).T.astype(jnp.bfloat16)
    return (forward_z, scaled_z, plain_z, forward_y, inverse_y, cosine_x, sine_x)


def to_modes(field_part, tables):
    forward_z, scaled_z, plain_z, forward_y, inverse_y, cosine_x, sine_x = tables
    channels = field_part.shape[0]
    planes = field_part.shape[1]
    grid_view = field_part.reshape(channels, planes, NY, NZ)
    section_one = jnp.einsum(
        "cxyz,zpk->cxkpy", grid_view, forward_z, preferred_element_type=jnp.float32
    ).astype(jnp.bfloat16)
    section_one = section_one.reshape(channels, planes, MZ, 2 * NY)
    section_two = jnp.einsum(
        "cxkm,mn->cxkn", section_one, forward_y, preferred_element_type=jnp.float32
    ).astype(jnp.bfloat16)
    section_two = section_two.reshape(channels, planes, 2 * MZ * MY)
    pencils = lax.all_to_all(section_two, "slab", split_axis=2, concat_axis=1, tiled=True)
    pencils = pencils.reshape(channels, NX, -1, 2)
    along_cos = jnp.einsum("cxmq,xk->cmqk", pencils, cosine_x, preferred_element_type=jnp.float32)
    along_sin = jnp.einsum("cxmq,xk->cmqk", pencils, sine_x, preferred_element_type=jnp.float32)
    real_part = along_cos[:, :, 0] + along_sin[:, :, 1]
    imag_part = along_cos[:, :, 1] - along_sin[:, :, 0]
    return jnp.stack([real_part, imag_part], 2)


def to_grid(spectra, tables, table_z):
    forward_z, scaled_z, plain_z, forward_y, inverse_y, cosine_x, sine_x = tables
    channels = spectra.shape[0]
    back_cos = jnp.einsum("cmqk,xk->cxmq", spectra, cosine_x, preferred_element_type=jnp.float32)
    back_sin = jnp.einsum("cmqk,xk->cxmq", spectra, sine_x, preferred_element_type=jnp.float32)
    real_part = back_cos[..., 0] - back_sin[..., 1]
    imag_part = back_cos[..., 1] + back_sin[..., 0]
    pencil_rows = jnp.stack([real_part, imag_part], -1).astype(jnp.bfloat16)
    pencil_rows = pencil_rows.reshape(channels, NX, -1)
    slabs = lax.all_to_all(pencil_rows, "slab", split_axis=1, concat_axis=2, tiled=True)
    channels = slabs.shape[0]
    planes = slabs.shape[1]
    slabs = slabs.reshape(channels, planes, MZ, 2 * MY)
    section_two = jnp.einsum(
        "cxkn,nm->cxkm", slabs, inverse_y, preferred_element_type=jnp.float32
    ).astype(jnp.bfloat16)
    section_two = section_two.reshape(channels, planes, MZ, 2, NY)
    grid_view = jnp.einsum(
        "cxkpy,kpz->cxyz", section_two, table_z, preferred_element_type=jnp.float32
    )
    return grid_view.reshape(channels, planes, NY * NZ)


def gelu_grad(pre_act):
    normal_cdf = 0.5 * (1.0 + jax.scipy.special.erf(pre_act / math.sqrt(2.0)))
    normal_pdf = jnp.exp(-0.5 * pre_act * pre_act) / math.sqrt(2.0 * math.pi)
    return normal_cdf + pre_act * normal_pdf


def body(field, cotangent, spectral_weight, point_weight, point_bias):
    tables = make_tables()
    scaled_z = tables[1]
    plain_z = tables[2]
    group_size = spectral_weight.shape[1]
    modes_dev = spectral_weight.shape[3]
    chan_start = lax.axis_index("chan") * group_size
    own_field = lax.dynamic_slice_in_dim(field, chan_start, group_size, 0)
    coeff = to_modes(own_field, tables).astype(jnp.bfloat16)
    coeff_real = coeff[:, :, 0]
    coeff_imag = coeff[:, :, 1]
    real_weight = spectral_weight[0]
    imag_weight = spectral_weight[1]
    spec_real = jnp.einsum(
        "imk,iomk->omk", coeff_real, real_weight, preferred_element_type=jnp.float32
    ) - jnp.einsum("imk,iomk->omk", coeff_imag, imag_weight, preferred_element_type=jnp.float32)
    spec_imag = jnp.einsum(
        "imk,iomk->omk", coeff_real, imag_weight, preferred_element_type=jnp.float32
    ) + jnp.einsum("imk,iomk->omk", coeff_imag, real_weight, preferred_element_type=jnp.float32)
    partial_spectra = jnp.stack([spec_real, spec_imag], 2)
    spectra = lax.psum(partial_spectra.astype(jnp.bfloat16), "chan")
    shaped = to_grid(spectra, tables, scaled_z)
    mixed = jnp.einsum("io,ixc->oxc", point_weight, field, preferred_element_type=jnp.float32)
    pre_act = shaped + mixed + point_bias.astype(jnp.float32)[:, None, None]
    grad_pre = (cotangent.astype(jnp.float32) * gelu_grad(pre_act)).astype(jnp.bfloat16)
    mode_index = lax.axis_index("slab") * modes_dev + jnp.arange(modes_dev, dtype=jnp.int32)
    mode_scale = (jnp.where(mode_index // MY == 0, 1.0, 2.0) / (NX * NY * NZ)).astype(jnp.float32)
    grad_hat = (to_modes(grad_pre, tables) * mode_scale[None, :, None, None]).astype(jnp.bfloat16)
    grad_real = grad_hat[:, :, 0]
    grad_imag = grad_hat[:, :, 1]
    outer_real = jnp.einsum(
        "imk,omk->iomk", coeff_real, grad_real, preferred_element_type=jnp.float32
    ) + jnp.einsum("imk,omk->iomk", coeff_imag, grad_imag, preferred_element_type=jnp.float32)
    outer_imag = jnp.einsum(
        "imk,omk->iomk", coeff_real, grad_imag, preferred_element_type=jnp.float32
    ) - jnp.einsum("imk,omk->iomk", coeff_imag, grad_real, preferred_element_type=jnp.float32)
    grad_spectral = jnp.stack([outer_real, outer_imag], 0)
    adj_real = jnp.einsum(
        "omk,iomk->imk", grad_real, real_weight, preferred_element_type=jnp.float32
    ) + jnp.einsum("omk,iomk->imk", grad_imag, imag_weight, preferred_element_type=jnp.float32)
    adj_imag = jnp.einsum(
        "omk,iomk->imk", grad_imag, real_weight, preferred_element_type=jnp.float32
    ) - jnp.einsum("omk,iomk->imk", grad_real, imag_weight, preferred_element_type=jnp.float32)
    adjoint = jnp.stack([adj_real, adj_imag], 2).astype(jnp.bfloat16)
    spectral_back = to_grid(adjoint, tables, plain_z)
    own_rows = lax.dynamic_slice_in_dim(point_weight, chan_start, group_size, 0)
    point_back = jnp.einsum("io,oxc->ixc", own_rows, grad_pre, preferred_element_type=jnp.float32)
    grad_input = (spectral_back + point_back).astype(jnp.bfloat16)
    inverse_root = 1.0 / math.sqrt(NX * NY * NZ)
    weight_part = (
        jnp.einsum("ixc,oxc->io", own_field, grad_pre, preferred_element_type=jnp.float32)
        * inverse_root
    )
    bias_part = jnp.sum(grad_pre, axis=(1, 2), dtype=jnp.float32) * inverse_root
    grad_pointwise, grad_bias = lax.psum((weight_part, bias_part), "slab")
    return (grad_input, grad_spectral, grad_pointwise, grad_bias)


def solution(mesh):
    placed = (
        P(None, "slab", None),
        P(None, "slab", None),
        P(None, "chan", None, "slab", None),
        P(),
        P(),
    )
    return jax.shard_map(
        body,
        mesh=mesh,
        in_specs=placed,
        out_specs=(
            P("chan", "slab", None),
            P(None, "chan", None, "slab", None),
            P("chan", None),
            P(),
        ),
        check_vma=False,
    )
```

profile of v0, /device:TPU:1, one launch (start us, length us, event | category | flops | bytes accessed | tf_op | source)
XLA Modules:
  0.0 397.6 jit_solution(5632324393416578759)
XLA Ops:
  1.1 1.8 copy.125
  3.6 0.6 fusion.17
  4.8 0.5 copy.181
  5.2 1.0 reshape.605
  6.2 18.4 %all-to-all-start = ((bf16[128,2,128]{2,1,0:T(2,128)(2,1)}), bf16[128,2,128]{2,1,0:T(2,128)(2,1)S(1)}, u32[]{:S(2)}, u32[]{:S(2)}) async-start(bf16[128,2,128]{2,1,0:T(2,128)(2,1)} %reshape.605), calls=%async_computation | async-start | bytes 131072 | tf_op jit(solution)/shard_map/all_to_all | solution.py:64
  25.2 10.9 %all-to-all-done = bf16[128,2,128]{2,1,0:T(2,128)(2,1)S(1)} async-done(((bf16[128,2,128]{2,1,0:T(2,128)(2,1)}), bf16[128,2,128]{2,1,0:T(2,128)(2,1)S(1)}, u32[]{:S(2)}, u32[]{:S(2)}) %all-to-all-start) | async-done | bytes 65568 | tf_op jit(solution)/shard_map/all_to_all | solution.py:64
  36.6 0.4 copy.132
  39.8 13.8 %psum.21 = bf16[64,4,2,32]{0,3,2,1:T(8,128)(2,1)S(1)} all-reduce(bf16[64,4,2,32]{0,3,2,1:T(8,128)(2,1)S(1)} %pad_maximum_fusion.2), channel_id=1, replica_groups=mesh['slab'=128,'chan'=4] {'chan'}, use_global_device_ids=true, to_apply=%region_0.1 | all-reduce | flops 16384 | bytes 65536 | tf_op jit(solution)/shard_map/psum | solution.py:122
  54.8 1.0 reshape.607
  55.8 9.5 %all-to-all-start.1 = ((bf16[128,2,512]{2,1,0:T(2,128)(2,1)}), bf16[128,2,512]{2,1,0:T(2,128)(2,1)S(1)}, u32[]{:S(2)}, u32[]{:S(2)}) async-start(bf16[128,2,512]{2,1,0:T(2,128)(2,1)} %reshape.607), calls=%async_computation.1 | async-start | bytes 524288 | tf_op jit(solution)/shard_map/all_to_all | solution.py:82
  65.5 15.2 %all-to-all-done.1 = bf16[128,2,512]{2,1,0:T(2,128)(2,1)S(1)} async-done(((bf16[128,2,512]{2,1,0:T(2,128)(2,1)}), bf16[128,2,512]{2,1,0:T(2,128)(2,1)S(1)}, u32[]{:S(2)}, u32[]{:S(2)}) %all-to-all-start.1) | async-done | bytes 262176 | tf_op jit(solution)/shard_map/all_to_all | solution.py:82
  81.0 0.8 copy.137
  82.5 2.7 convolution_bitcast_fusion
  85.2 4.2 %reshape.568 = f32[64,2,4096]{2,1,0:T(2,128)S(1)} reshape(f32[64,2,64,64]{3,2,1,0:T(8,128)} %convolution_bitcast_fusion) | data formatting | bytes 4194304 | tf_op jit(solution)/shard_map/reshape | solution.py:93
  89.4 5.7 %convert_reduce_fusion = (f32[64]{0:T(128)S(1)}, bf16[64,2,4096]{2,0,1:T(8,128)(2,1)S(1)}) fusion(f32[64]{0:T(128)S(1)} %convert_element_type.232, bf16[64,2,4096]{2,1,0:T(2,128)(2,1)} %param.5, bf16[64,64]{1,0:T(8,128)(2,1)S(1)} %copy-done, f32[64,2,4096]{2,1,0:T(2,128)S(1)} %reshape.568, bf16[64,2,4096]{2,1,0:T(2,128)(2,1)} %param.6), kind=kOutput, calls=%fused_computation.16 | convolution fusion | flops 74973120 | bytes 5251584 | tf_op jit(solution)/shard_map/io,ixc->oxc/dot_general | solution.py:124
  95.1 2.3 reshape.569
  97.4 2.0 fusion.14
  99.4 1.6 copy.143
  101.1 0.5 reshape.570
  101.9 0.7 copy.183
  102.6 1.0 reshape.609
  103.6 5.8 %all-to-all-start.2 = ((bf16[128,2,512]{2,1,0:T(2,128)(2,1)}), bf16[128,2,512]{2,1,0:T(2,128)(2,1)S(1)}, u32[]{:S(2)}, u32[]{:S(2)}) async-start(bf16[128,2,512]{2,1,0:T(2,128)(2,1)} %reshape.609), calls=%async_computation.2 | async-start | bytes 524288 | tf_op jit(solution)/shard_map/all_to_all | solution.py:64
  109.8 256.7 %all-reduce = (f32[16,64]{1,0:T(8,128)}, f32[64]{0:T(128)}) all-reduce(f32[16,64]{1,0:T(8,128)S(1)} %fusion.18, f32[64]{0:T(128)S(1)} %broadcast_multiply_fusion), channel_id=1, replica_groups=mesh['slab'=128,'chan'=4] {'slab'}, use_global_device_ids=true, to_apply=%region_1.2 | all-reduce | flops 1088 | bytes 8704 | tf_op jit(solution)/shard_map/psum | solution.py:156
  367.0 0.5 copy.147
  369.2 0.4 fusion.30
  371.5 1.0 reshape.611
  372.5 10.4 %all-to-all-start.3 = ((bf16[128,2,128]{2,1,0:T(2,128)(2,1)}), bf16[128,2,128]{2,1,0:T(2,128)(2,1)S(1)}, u32[]{:S(2)}, u32[]{:S(2)}) async-start(bf16[128,2,128]{2,1,0:T(2,128)(2,1)} %reshape.611), calls=%async_computation.3 | async-start | bytes 131072 | tf_op jit(solution)/shard_map/all_to_all | solution.py:82
  382.9 0.6 add_bitcast_fusion
  383.5 1.6 pad_maximum_fusion
  385.1 9.2 %all-to-all-done.3 = bf16[128,2,128]{2,1,0:T(2,128)(2,1)S(1)} async-done(((bf16[128,2,128]{2,1,0:T(2,128)(2,1)}), bf16[128,2,128]{2,1,0:T(2,128)(2,1)S(1)}, u32[]{:S(2)}, u32[]{:S(2)}) %all-to-all-start.3) | async-done | bytes 65568 | tf_op jit(solution)/shard_map/all_to_all | solution.py:82
  395.7 0.5 reshape.575
  396.6 1.0 copy.156
  (99 shorter events, 14.1 us)
Async XLA Ops:
  0.6 88.8 %copy-start = (bf16[64,64]{1,0:T(8,128)(2,1)S(1)}, bf16[64,64]{1,0:T(8,128)(2,1)}, u32[]{:S(2)}) copy-start(bf16[64,64]{1,0:T(8,128)(2,1)} %param.8) | copy-start | bytes 24580
  3.2 21.6 %copy-start.1 = (bf16[2,16,64,4,32]{2,4,3,1,0:T(8,128)(2,1)S(1)}, bf16[2,16,64,4,32]{2,4,3,1,0:T(8,128)(2,1)}, u32[]{:S(2)}) copy-start(bf16[2,16,64,4,32]{2,4,3,1,0:T(8,128)(2,1)} %param.7) | copy-start | bytes 1572868
  4.6 20.5 %copy-start.6 = (bf16[64]{0:T(256)(128)(2,1)S(1)}, bf16[64]{0:T(256)(128)(2,1)}, u32[]{:S(2)}) copy-start(bf16[64]{0:T(256)(128)(2,1)} %param.9) | copy-start | bytes 388
  6.2 29.8 %all-to-all-start = ((bf16[128,2,128]{2,1,0:T(2,128)(2,1)}), bf16[128,2,128]{2,1,0:T(2,128)(2,1)S(1)}, u32[]{:S(2)}, u32[]{:S(2)}) async-start(bf16[128,2,128]{2,1,0:T(2,128)(2,1)} %reshape.605), calls=%async_computation | async-start | bytes 131072 | tf_op jit(solution)/shard_map/all_to_all | solution.py:64
  24.9 13.9 %copy-start.2 = (bf16[16,64,4,32]{1,3,2,0:T(8,128)(2,1)}, bf16[16,64,4,32]{1,3,2,0:T(8,128)(2,1)S(1)}, u32[]{:S(2)}) copy-start(bf16[16,64,4,32]{1,3,2,0:T(8,128)(2,1)S(1)} %get-tuple-element.33) | copy-start | bytes 786436
  24.9 14.3 %copy-start.4 = (bf16[16,64,4,32]{1,3,2,0:T(8,128)(2,1)}, bf16[16,64,4,32]{1,3,2,0:T(8,128)(2,1)S(1)}, u32[]{:S(2)}) copy-start(bf16[16,64,4,32]{1,3,2,0:T(8,128)(2,1)S(1)} %get-tuple-element.32) | copy-start | bytes 786436
  55.8 24.8 %all-to-all-start.1 = ((bf16[128,2,512]{2,1,0:T(2,128)(2,1)}), bf16[128,2,512]{2,1,0:T(2,128)(2,1)S(1)}, u32[]{:S(2)}, u32[]{:S(2)}) async-start(bf16[128,2,512]{2,1,0:T(2,128)(2,1)} %reshape.607), calls=%async_computation.1 | async-start | bytes 524288 | tf_op jit(solution)/shard_map/all_to_all | solution.py:82
  103.6 262.9 %all-to-all-start.2 = ((bf16[128,2,512]{2,1,0:T(2,128)(2,1)}), bf16[128,2,512]{2,1,0:T(2,128)(2,1)S(1)}, u32[]{:S(2)}, u32[]{:S(2)}) async-start(bf16[128,2,512]{2,1,0:T(2,128)(2,1)} %reshape.609), calls=%async_computation.2 | async-start | bytes 524288 | tf_op jit(solution)/shard_map/all_to_all | solution.py:64
  366.8 1.5 copy-start.3
  366.9 1.9 copy-start.5
  372.5 21.8 %all-to-all-start.3 = ((bf16[128,2,128]{2,1,0:T(2,128)(2,1)}), bf16[128,2,128]{2,1,0:T(2,128)(2,1)S(1)}, u32[]{:S(2)}, u32[]{:S(2)}) async-start(bf16[128,2,128]{2,1,0:T(2,128)(2,1)} %reshape.611), calls=%async_computation.3 | async-start | bytes 131072 | tf_op jit(solution)/shard_map/all_to_all | solution.py:82
where the time goes:
time: 398 us
  blocking collectives  270 us (68%)
  starting transfers between devices  44.1 us (11%)
  waiting for transfers between devices  35.3 us (9%)
  local copies, waits for them, and re-layouts  24 us (6%)
  matrix products  19.2 us (5%)
    psum x1, blocking collectives, body(): grad_pointwise, grad_bias = lax.psum((weight_part, bias_part), 'slab')  257 us
    all_to_all x2, waiting for transfers between devices, to_grid(): lax.all_to_all(pencil_rows, 'slab', split_axis=1, concat_axis=2, tiled=True)  24.4 us
    all_to_all x2, starting transfers between devices, to_modes(): lax.all_to_all(section_two, 'slab', split_axis=2, concat_axis=1, tiled=True)  24.2 us
    all_to_all x2, starting transfers between devices, to_grid(): lax.all_to_all(pencil_rows, 'slab', split_axis=1, concat_axis=2, tiled=True)  19.9 us
    psum x1, blocking collectives, body(): spectra = lax.psum(partial_spectra.astype(jnp.bfloat16), 'chan')  13.8 us
    all_to_all x2, waiting for transfers between devices, to_modes(): lax.all_to_all(section_two, 'slab', split_axis=2, concat_axis=1, tiled=True)  10.9 us
    unnamed x24, local copies, waits for them, and re-layouts  8.16 us
  transfers between devices with their start and end apart: 4, of which 3 were waited for; matrix products, arithmetic and copies ran while one was open for 1% of the time, Pallas kernels for 0%

commit v1 on v0

--- a/solution.py
+++ b/solution.py
@@ -10,6 +10,10 @@
 NX = 256
 NY = 64
 NZ = 64
+
+
+def read_meshes_on_mesh(patch, named_axis):
+    return jnp.sum(lax.all_gather(patch, named_axis), axis=0)
 
 
 def kept_modes(total, length):
@@ -119,7 +123,7 @@
         "imk,iomk->omk", coeff_real, imag_weight, preferred_element_type=jnp.float32
     ) + jnp.einsum("imk,iomk->omk", coeff_imag, real_weight, preferred_element_type=jnp.float32)
     partial_spectra = jnp.stack([spec_real, spec_imag], 2)
-    spectra = lax.psum(partial_spectra.astype(jnp.bfloat16), "chan")
+    spectra = read_meshes_on_mesh(partial_spectra.astype(jnp.bfloat16), "chan")
     shaped = to_grid(spectra, tables, scaled_z)
     mixed = jnp.einsum("io,ixc->oxc", point_weight, field, preferred_element_type=jnp.float32)
     pre_act = shaped + mixed + point_bias.astype(jnp.float32)[:, None, None]

time: 398 us -> 393 us (0.987)
    psum x1 -> x0, blocking collectives: 13.8 us -> none  [body(): spectra = lax.psum(partial_spectra.astype(jnp.bfloat16), 'chan')]
    all_gather x0 -> x1, blocking collectives: none -> 10.1 us  [read_meshes_on_mesh(): return jnp.sum(lax.all_gather(patch, named_axis), axis=0)]
where the time goes in v1:
time: 393 us
  blocking collectives  267 us (68%)
  starting transfers between devices  42.9 us (11%)
  waiting for transfers between devices  35.3 us (9%)
  local copies, waits for them, and re-layouts  24 us (6%)
  matrix products  19.2 us (5%)
    psum x1, blocking collectives, body(): grad_pointwise, grad_bias = lax.psum((weight_part, bias_part), 'slab')  257 us
    all_to_all x2, waiting for transfers between devices, to_grid(): lax.all_to_all(pencil_rows, 'slab', split_axis=1, concat_axis=2, tiled=True)  24.4 us
    all_to_all x2, starting transfers between devices, to_modes(): lax.all_to_all(section_two, 'slab', split_axis=2, concat_axis=1, tiled=True)  24.2 us
    all_to_all x2, starting transfers between devices, to_grid(): lax.all_to_all(pencil_rows, 'slab', split_axis=1, concat_axis=2, tiled=True)  18.7 us
    all_to_all x2, waiting for transfers between devices, to_modes(): lax.all_to_all(section_two, 'slab', split_axis=2, concat_axis=1, tiled=True)  10.9 us
    all_gather x1, blocking collectives, read_meshes_on_mesh(): return jnp.sum(lax.all_gather(patch, named_axis), axis=0)  10.1 us
    unnamed x24, local copies, waits for them, and re-layouts  8.17 us
  transfers between devices with their start and end apart: 4, of which 3 were waited for; matrix products, arithmetic and copies ran while one was open for 1% of the time, Pallas kernels for 0%

profile of v1, /device:TPU:1, one launch (start us, length us, event | category | flops | bytes accessed | tf_op | source)
XLA Modules:
  0.0 392.8 jit_solution(692338109514496224)
XLA Ops:
  1.1 1.8 copy.125
  3.6 0.6 fusion.17
  4.8 0.5 copy.181
  5.2 1.0 reshape.638
  6.2 18.4 %all-to-all-start = ((bf16[128,2,128]{2,1,0:T(2,128)(2,1)}), bf16[128,2,128]{2,1,0:T(2,128)(2,1)S(1)}, u32[]{:S(2)}, u32[]{:S(2)}) async-start(bf16[128,2,128]{2,1,0:T(2,128)(2,1)} %reshape.638), calls=%async_computation | async-start | bytes 131072 | tf_op jit(solution)/shard_map/all_to_all | solution.py:68
  25.1 10.9 %all-to-all-done = bf16[128,2,128]{2,1,0:T(2,128)(2,1)S(1)} async-done(((bf16[128,2,128]{2,1,0:T(2,128)(2,1)}), bf16[128,2,128]{2,1,0:T(2,128)(2,1)S(1)}, u32[]{:S(2)}, u32[]{:S(2)}) %all-to-all-start) | async-done | bytes 65568 | tf_op jit(solution)/shard_map/all_to_all | solution.py:68
  36.6 0.4 copy.132
  39.7 10.1 %all_gather.4 = bf16[4,64,4,2,32]{1,4,3,2,0:T(8,128)(2,1)S(1)} all-gather(bf16[1,64,4,2,32]{1,4,3,2,0:T(8,128)(2,1)S(1)} %pad_maximum_fusion.2), channel_id=1, replica_groups=mesh['slab'=128,'chan'=4] {'chan'}, dimensions={0}, use_global_device_ids=true | all-gather | bytes 163840 | tf_op jit(solution)/shard_map/all_gather | solution.py:16
  51.1 1.0 reshape.640
  52.1 8.3 %all-to-all-start.1 = ((bf16[128,2,512]{2,1,0:T(2,128)(2,1)}), bf16[128,2,512]{2,1,0:T(2,128)(2,1)S(1)}, u32[]{:S(2)}, u32[]{:S(2)}) async-start(bf16[128,2,512]{2,1,0:T(2,128)(2,1)} %reshape.640), calls=%async_computation.1 | async-start | bytes 524288 | tf_op jit(solution)/shard_map/all_to_all | solution.py:86
  60.6 15.2 %all-to-all-done.1 = bf16[128,2,512]{2,1,0:T(2,128)(2,1)S(1)} async-done(((bf16[128,2,512]{2,1,0:T(2,128)(2,1)}), bf16[128,2,512]{2,1,0:T(2,128)(2,1)S(1)}, u32[]{:S(2)}, u32[]{:S(2)}) %all-to-all-start.1) | async-done | bytes 262176 | tf_op jit(solution)/shard_map/all_to_all | solution.py:86
  76.2 0.8 copy.137
  77.7 2.7 convolution_bitcast_fusion
  80.4 4.2 %reshape.601 = f32[64,2,4096]{2,1,0:T(2,128)S(1)} reshape(f32[64,2,64,64]{3,2,1,0:T(8,128)} %convolution_bitcast_fusion) | data formatting | bytes 4194304 | tf_op jit(solution)/shard_map/reshape | solution.py:97
  84.6 5.7 %convert_reduce_fusion = (f32[64]{0:T(128)S(1)}, bf16[64,2,4096]{2,0,1:T(8,128)(2,1)S(1)}) fusion(f32[64]{0:T(128)S(1)} %convert_element_type.241, bf16[64,2,4096]{2,1,0:T(2,128)(2,1)} %param.5, bf16[64,64]{1,0:T(8,128)(2,1)S(1)} %copy-done, f32[64,2,4096]{2,1,0:T(2,128)S(1)} %reshape.601, bf16[64,2,4096]{2,1,0:T(2,128)(2,1)} %param.6), kind=kOutput, calls=%fused_computation.16 | convolution fusion | flops 74973120 | bytes 5251584 | tf_op jit(solution)/shard_map/io,ixc->oxc/dot_general | solution.py:128
  90.3 2.3 reshape.602
  92.6 2.0 fusion.14
  94.6 1.6 copy.143
  96.2 0.5 reshape.603
  97.0 0.7 copy.183
  97.7 1.0 reshape.642
  98.7 5.8 %all-to-all-start.2 = ((bf16[128,2,512]{2,1,0:T(2,128)(2,1)}), bf16[128,2,512]{2,1,0:T(2,128)(2,1)S(1)}, u32[]{:S(2)}, u32[]{:S(2)}) async-start(bf16[128,2,512]{2,1,0:T(2,128)(2,1)} %reshape.642), calls=%async_computation.2 | async-start | bytes 524288 | tf_op jit(solution)/shard_map/all_to_all | solution.py:68
  105.0 256.7 %all-reduce = (f32[16,64]{1,0:T(8,128)}, f32[64]{0:T(128)}) all-reduce(f32[16,64]{1,0:T(8,128)S(1)} %fusion.18, f32[64]{0:T(128)S(1)} %broadcast_multiply_fusion), channel_id=1, replica_groups=mesh['slab'=128,'chan'=4] {'slab'}, use_global_device_ids=true, to_apply=%region_1.2 | all-reduce | flops 1088 | bytes 8704 | tf_op jit(solution)/shard_map/psum | solution.py:160
  362.2 0.5 copy.147
  364.8 0.4 fusion.20
  366.7 1.0 reshape.644
  367.6 10.4 %all-to-all-start.3 = ((bf16[128,2,128]{2,1,0:T(2,128)(2,1)}), bf16[128,2,128]{2,1,0:T(2,128)(2,1)S(1)}, u32[]{:S(2)}, u32[]{:S(2)}) async-start(bf16[128,2,128]{2,1,0:T(2,128)(2,1)} %reshape.644), calls=%async_computation.3 | async-start | bytes 131072 | tf_op jit(solution)/shard_map/all_to_all | solution.py:86
  378.0 0.6 add_bitcast_fusion
  378.7 1.6 pad_maximum_fusion
  380.2 9.2 %all-to-all-done.3 = bf16[128,2,128]{2,1,0:T(2,128)(2,1)S(1)} async-done(((bf16[128,2,128]{2,1,0:T(2,128)(2,1)}), bf16[128,2,128]{2,1,0:T(2,128)(2,1)S(1)}, u32[]{:S(2)}, u32[]{:S(2)}) %all-to-all-start.3) | async-done | bytes 65568 | tf_op jit(solution)/shard_map/all_to_all | solution.py:86
  390.8 0.5 reshape.608
  391.8 1.0 copy.156
  (100 shorter events, 14.2 us)
Async XLA Ops:
  0.6 84.0 %copy-start = (bf16[64,64]{1,0:T(8,128)(2,1)S(1)}, bf16[64,64]{1,0:T(8,128)(2,1)}, u32[]{:S(2)}) copy-start(bf16[64,64]{1,0:T(8,128)(2,1)} %param.8) | copy-start | bytes 24580
  3.2 21.6 %copy-start.1 = (bf16[2,16,64,4,32]{2,4,3,1,0:T(8,128)(2,1)S(1)}, bf16[2,16,64,4,32]{2,4,3,1,0:T(8,128)(2,1)}, u32[]{:S(2)}) copy-start(bf16[2,16,64,4,32]{2,4,3,1,0:T(8,128)(2,1)} %param.7) | copy-start | bytes 1572868
  4.6 20.5 %copy-start.6 = (bf16[64]{0:T(256)(128)(2,1)S(1)}, bf16[64]{0:T(256)(128)(2,1)}, u32[]{:S(2)}) copy-start(bf16[64]{0:T(256)(128)(2,1)} %param.9) | copy-start | bytes 388
  6.2 29.8 %all-to-all-start = ((bf16[128,2,128]{2,1,0:T(2,128)(2,1)}), bf16[128,2,128]{2,1,0:T(2,128)(2,1)S(1)}, u32[]{:S(2)}, u32[]{:S(2)}) async-start(bf16[128,2,128]{2,1,0:T(2,128)(2,1)} %reshape.638), calls=%async_computation | async-start | bytes 131072 | tf_op jit(solution)/shard_map/all_to_all | solution.py:68
  24.9 13.9 %copy-start.2 = (bf16[16,64,4,32]{1,3,2,0:T(8,128)(2,1)}, bf16[16,64,4,32]{1,3,2,0:T(8,128)(2,1)S(1)}, u32[]{:S(2)}) copy-start(bf16[16,64,4,32]{1,3,2,0:T(8,128)(2,1)S(1)} %get-tuple-element.33) | copy-start | bytes 786436
  24.9 14.4 %copy-start.4 = (bf16[16,64,4,32]{1,3,2,0:T(8,128)(2,1)}, bf16[16,64,4,32]{1,3,2,0:T(8,128)(2,1)S(1)}, u32[]{:S(2)}) copy-start(bf16[16,64,4,32]{1,3,2,0:T(8,128)(2,1)S(1)} %get-tuple-element.32) | copy-start | bytes 786436
  52.1 23.6 %all-to-all-start.1 = ((bf16[128,2,512]{2,1,0:T(2,128)(2,1)}), bf16[128,2,512]{2,1,0:T(2,128)(2,1)S(1)}, u32[]{:S(2)}, u32[]{:S(2)}) async-start(bf16[128,2,512]{2,1,0:T(2,128)(2,1)} %reshape.640), calls=%async_computation.1 | async-start | bytes 524288 | tf_op jit(solution)/shard_map/all_to_all | solution.py:86
  98.7 262.9 %all-to-all-start.2 = ((bf16[128,2,512]{2,1,0:T(2,128)(2,1)}), bf16[128,2,512]{2,1,0:T(2,128)(2,1)S(1)}, u32[]{:S(2)}, u32[]{:S(2)}) async-start(bf16[128,2,512]{2,1,0:T(2,128)(2,1)} %reshape.642), calls=%async_computation.2 | async-start | bytes 524288 | tf_op jit(solution)/shard_map/all_to_all | solution.py:68
  362.0 1.5 copy-start.3
  362.1 1.9 copy-start.5
  367.6 21.8 %all-to-all-start.3 = ((bf16[128,2,128]{2,1,0:T(2,128)(2,1)}), bf16[128,2,128]{2,1,0:T(2,128)(2,1)S(1)}, u32[]{:S(2)}, u32[]{:S(2)}) async-start(bf16[128,2,128]{2,1,0:T(2,128)(2,1)} %reshape.644), calls=%async_computation.3 | async-start | bytes 131072 | tf_op jit(solution)/shard_map/all_to_all | solution.py:86
